TPU v7x, 512 devices: a whole 4x8x8 slice. The times are simulated.
512 devices in a mesh: band: 4 (over x), ty: 16 (over y, core), tx: 8 (over z).
Axes of the slice: x: 4, y: 8, z: 8, core: 2. Of those that a mesh axis runs over, the one named last changes fastest.
Arguments:
- dirty: float32 [8, 4096, 2048], P('band', 'ty', 'tx'), may hold values from -6 to 6
- psf: bfloat16 [8, 20, 2304], P('band'), may hold values from -4 to 4
- comp_tile: int32 [16384, 1], P(('ty', 'tx')), may hold values from 0 to 127; in each aligned block of 128 rows (0 to 127, 128 to 255, ...) at most 2 rows name the same one
- comp_offset: int32 [16384, 2], P(('ty', 'tx')), may hold values from 0 to 255
- comp_scale: int32 [16384], P(('ty', 'tx')), may hold values from 0 to 4
- comp_amp: float32 [16384, 4], P(('ty', 'tx')), may hold values from -6 to 6
- fit_weight: float32 [8, 4], P('band'), may hold values from -5 to 5
Outputs:
- residual: float32 [8, 4096, 2048], P('band', 'ty', 'tx')
- taylor_fit: float32 [4, 4096, 2048], P('band', 'ty', 'tx')
Inputs may be any that keep to these rules, and one draw needn't show every extreme that they name: `comp_tile`: the 128 components of one device name at most 2 components for one tile, and exactly 2 for some tile on some device.
All inputs are finite; a program needn't handle non-finite values.
Results may differ from a plain program's by a relative error of at most 0.0022.
Values may be sent and summed in bfloat16 or wider, within the bound.
A program may use at most 64 MiB of HBM per device.

v0:
```python
import jax
import jax.numpy as jnp
from jax import lax
from jax.sharding import PartitionSpec as P

TAYLOR = 4
SCALES = 5
PATCH = 48


def passed_along(value, axis, steps):
    count = lax.axis_size(axis)
    initial, last = (max(0, -steps), min(count, count - steps))
    return lax.ppermute(value, axis, [(source, source + steps) for source in range(initial, last)])


def make_patches(amps, scales, psf_local):
    count = amps.shape[0]
    select = (scales[:, None] == jnp.arange(SCALES, dtype=jnp.int32)[None, :]).astype(jnp.float32)
    coef = (amps[:, :, None] * select[:, None, :]).reshape(count, TAYLOR * SCALES)
    built = jnp.einsum(
        "sk,bkp->sbp", coef, psf_local.astype(jnp.float32), precision=lax.Precision.HIGHEST
    )
    return built.astype(jnp.bfloat16)


def pick_rows(onehot, values):
    return jnp.sum(
        jnp.where(onehot[:, :, None], values[None, :, :], jnp.zeros((), values.dtype)), axis=1
    )


def render(getter, slots, bands_here, height, width):
    block = 16
    span = jnp.arange(PATCH, dtype=jnp.int32)
    row_ids = jnp.arange(height, dtype=jnp.int32)
    col_ids = jnp.arange(width, dtype=jnp.int32)

    def step(index, model):
        patch_blk, offs_blk = getter(index * block)
        patch_four = patch_blk.reshape(block, bands_here, PATCH, PATCH)
        col_table = (
            col_ids[None, None, :] == offs_blk[:, 1][:, None, None] + span[None, :, None]
        ).astype(jnp.bfloat16)
        placed = jnp.einsum(
            "cbuv,cvw->bcuw", patch_four, col_table, preferred_element_type=jnp.float32
        ).astype(jnp.bfloat16)
        row_table = (
            row_ids[:, None, None] == offs_blk[:, 0][None, :, None] + span[None, None, :]
        ).astype(jnp.bfloat16)
        row_table = row_table.reshape(height, block * PATCH)
        placed = placed.reshape(bands_here, block * PATCH, width)
        return model + jnp.einsum(
            "hk,bkw->bhw", row_table, placed, preferred_element_type=jnp.float32
        )

    start = jnp.zeros((bands_here, height, width), jnp.float32)
    return lax.fori_loop(0, slots // block, step, start)


def per_device(dirty, psf, comp_tile, comp_offset, comp_scale, comp_amp, fit_weight):
    bands_here = dirty.shape[0]
    tile_side = dirty.shape[1]
    height = tile_side + PATCH
    n_tiles = lax.axis_size("ty") * lax.axis_size("tx")
    listed = comp_tile.shape[0]
    cap_each = max(2, 2 * listed // n_tiles)
    slots = n_tiles * cap_each
    dest = comp_tile[:, 0]
    order = jnp.arange(listed, dtype=jnp.int32)
    same = (dest[:, None] == dest[None, :]) & (order[:, None] > order[None, :])
    rank = jnp.sum(same.astype(jnp.int32), axis=1)
    slot_of = dest * cap_each + rank
    onehot = jnp.arange(slots, dtype=jnp.int32)[:, None] == slot_of[None, :]
    offs_send = pick_rows(onehot, comp_offset)
    patches = make_patches(comp_amp, comp_scale, psf).reshape(listed, -1)
    send = jnp.dot(onehot.astype(jnp.bfloat16), patches, preferred_element_type=jnp.float32).astype(
        jnp.bfloat16
    )
    got, offs_got = (
        lax.all_to_all(send, ("ty", "tx"), split_axis=0, concat_axis=0, tiled=True),
        lax.all_to_all(offs_send, ("ty", "tx"), split_axis=0, concat_axis=0, tiled=True),
    )
    got = got.reshape(slots, bands_here, PATCH * PATCH)

    def getter(first):
        return (
            lax.dynamic_slice_in_dim(got, first, 16, 0),
            lax.dynamic_slice_in_dim(offs_got, first, 16, 0),
        )

    model = render(getter, slots, bands_here, height, height)
    right_strip = model[:, :, tile_side:].reshape(bands_here, -1)
    came_right = passed_along(right_strip, "tx", 1)
    model = model.at[:, :, :PATCH].add(came_right.reshape(bands_here, height, PATCH))
    model = model[:, :, :tile_side]
    lower_strip = model[:, tile_side:, :].reshape(bands_here, -1)
    came_lower = passed_along(lower_strip, "ty", 1)
    model = model.at[:, :PATCH, :].add(came_lower.reshape(bands_here, PATCH, tile_side))
    residual = dirty - model[:, :tile_side, :]
    taylor_fit = lax.psum_scatter(
        jnp.einsum("bt,byx->tyx", fit_weight, residual, precision=lax.Precision.HIGHEST),
        "band",
        scatter_dimension=0,
        tiled=True,
    )
    return (residual, taylor_fit)


def solution(mesh):
    return jax.shard_map(
        per_device,
        mesh=mesh,
        in_specs=(
            P("band", "ty", "tx"),
            P("band", None, None),
            P(("ty", "tx"), None),
            P(("ty", "tx"), None),
            P(("ty", "tx")),
            P(("ty", "tx"), None),
            P("band", None),
        ),
        out_specs=(P("band", "ty", "tx"), P("band", "ty", "tx")),
        check_vma=False,
    )
```

profile of v0, /device:TPU:32, one launch (start us, length us, event | category | flops | bytes accessed | tf_op | source)
XLA Modules:
  0.0 211.3 jit_solution(12639899799615487865)
XLA Ops:
  10.5 17.3 %all-to-all-start = ((s32[128,2,2]{1,2,0:T(2,128)}), s32[128,2,2]{1,2,0:T(2,128)S(1)}, u32[]{:S(2)}, u32[]{:S(2)}) async-start(s32[128,2,2]{1,2,0:T(2,128)} %copy.44), calls=%async_computation | async-start | bytes 262144 | tf_op jit(solution)/shard_map/all_to_all | solution.py:82
  30.4 1.4 copy.47
  31.8 2.0 convolution_convert_fusion.1
  33.8 2.3 %all_to_all.17 = bf16[128,2,4608]{2,1,0:T(2,128)(2,1)} reshape(bf16[256,4608]{1,0:T(8,128)(2,1)S(1)} %convolution_convert_fusion.1) | data formatting | bytes 4718592 | tf_op jit(solution)/shard_map/all_to_all | solution.py:81
  37.1 13.4 %all-to-all-start.1 = ((bf16[128,2,4608]{2,1,0:T(2,128)(2,1)}), bf16[128,2,4608]{2,1,0:T(2,128)(2,1)S(1)}, u32[]{:S(2)}, u32[]{:S(2)}) async-start(bf16[128,2,4608]{2,1,0:T(2,128)(2,1)} %all_to_all.17), calls=%async_computation.1 | async-start | bytes 4718592 | tf_op jit(solution)/shard_map/all_to_all | solution.py:81
  50.6 1.6 copy.45
  53.2 52.5 %all-to-all-done.1 = bf16[128,2,4608]{2,1,0:T(2,128)(2,1)S(1)} async-done(((bf16[128,2,4608]{2,1,0:T(2,128)(2,1)}), bf16[128,2,4608]{2,1,0:T(2,128)(2,1)S(1)}, u32[]{:S(2)}, u32[]{:S(2)}) %all-to-all-start.1) | async-done | bytes 2359328 | tf_op jit(solution)/shard_map/all_to_all | solution.py:81
  105.7 2.8 %reshape.232 = bf16[256,2,2304]{2,1,0:T(2,128)(2,1)} reshape(bf16[128,2,4608]{2,1,0:T(2,128)(2,1)S(1)} %all-to-all-done.1) | data formatting | bytes 4718592 | tf_op jit(solution)/shard_map/reshape | solution.py:84
  108.5 49.0 %while.18 = (s32[]{:T(128)}, f32[2,304,304]{1,2,0:T(8,128)S(1)}, s32[256,2]{0,1:T(2,128)S(1)}, bf16[256,2,2304]{2,1,0:T(2,128)(2,1)}, s32[]{:T(128)}, /*index=5*/s32[]{:T(128)}, s32[]{:T(128)}, s32[]{:T(128)}) while((s32[]{:T(128)}, f32[2,304,304]{1,2,0:T(8,128)S(1)}, s32[256,2]{0,1:T(2,128)S(1)}, ...), condition=%wide.region_3.4_spmd.clone.clone, body=%wide.region_2.3_spmd.clone.clone.sunk | while | flops 330033664 | bytes 2523925 | solution.py:58
  110.3 1.3 fusion.32
  116.4 1.3 fusion.32
  119.5 1.3 fusion.32
  122.5 1.3 fusion.32
  125.6 1.3 fusion.32
  128.7 1.3 fusion.32
  131.7 1.3 fusion.32
  144.0 1.3 fusion.32
  158.0 3.1 %collective-permute-start = (f32[2,14592]{1,0:T(2,128)S(1)}, f32[2,14592]{1,0:T(2,128)S(1)}, u32[]{:S(2)}, u32[]{:S(2)}) collective-permute-start(f32[2,14592]{1,0:T(2,128)S(1)} %reshape.233), channel_id=1, source_target_pairs={{0,1},{1,2},{2,3},{3,4},{4,5},{5,6},{6,7},{8,9},{9,10},{10,11},{11... | collective-permute-start | bytes 350216 | tf_op jit(solution)/shard_map/ppermute | solution.py:14
  161.4 2.0 collective-permute-done
  163.7 1.3 scatter-add.6
  165.1 2.1 collective-permute-start.1
  167.3 5.0 %collective-permute-done.1 = f32[2,12288]{1,0:T(2,128)S(1)} collective-permute-done((f32[2,12288]{1,0:T(2,128)S(1)}, f32[2,12288]{1,0:T(2,128)S(1)}, u32[]{:S(2)}, u32[]{:S(2)}) %collective-permute-start.1) | collective-permute-done | bytes 98336 | tf_op jit(solution)/shard_map/ppermute | solution.py:14
  172.4 2.1 convolution_bitcast_fusion
  175.7 28.8 %reduce-scatter.2.cloned.1.call-done = f32[1,256,256]{2,1,0:T(8,128)} async-done(((f32[4,256,256]{2,1,0:T(8,128)}), f32[1,256,256]{2,1,0:T(8,128)}) %reduce-scatter.2.cloned.1.call-update) | async-done | bytes 262160 | tf_op jit(solution)/shard_map/reduce_scatter | solution.py:101
  (141 shorter events, 48.3 us)
Async XLA Ops:
  7.2 22.1 %copy-start = (bf16[2,20,2304]{2,0,1:T(2,128)(2,1)S(1)}, bf16[2,20,2304]{2,0,1:T(2,128)(2,1)}, u32[]{:S(2)}) copy-start(bf16[2,20,2304]{2,0,1:T(2,128)(2,1)} %param.14) | copy-start | bytes 552964
  10.5 26.0 %all-to-all-start = ((s32[128,2,2]{1,2,0:T(2,128)}), s32[128,2,2]{1,2,0:T(2,128)S(1)}, u32[]{:S(2)}, u32[]{:S(2)}) async-start(s32[128,2,2]{1,2,0:T(2,128)} %copy.44), calls=%async_computation | async-start | bytes 262144 | tf_op jit(solution)/shard_map/all_to_all | solution.py:82
  36.5 0.7 copy-start.3
  37.1 68.6 %all-to-all-start.1 = ((bf16[128,2,4608]{2,1,0:T(2,128)(2,1)}), bf16[128,2,4608]{2,1,0:T(2,128)(2,1)S(1)}, u32[]{:S(2)}, u32[]{:S(2)}) async-start(bf16[128,2,4608]{2,1,0:T(2,128)(2,1)} %all_to_all.17), calls=%async_computation.1 | async-start | bytes 4718592 | tf_op jit(solution)/shard_map/all_to_all | solution.py:81
  50.5 153.9 %reduce-scatter.2.cloned.1.call-start = ((), (), s32[]{:S(2)}) async-start(), calls=%async_computation.3 | async-start | bytes 1310720 | tf_op jit(solution)/shard_map/reduce_scatter | solution.py:101
  158.0 5.5 %collective-permute-start = (f32[2,14592]{1,0:T(2,128)S(1)}, f32[2,14592]{1,0:T(2,128)S(1)}, u32[]{:S(2)}, u32[]{:S(2)}) collective-permute-start(f32[2,14592]{1,0:T(2,128)S(1)} %reshape.233), channel_id=1, source_target_pairs={{0,1},{1,2},{2,3},{3,4},{4,5},{5,6},{6,7},{8,9},{9,10},{10,11},{11... | collective-permute-start | bytes 350216 | tf_op jit(solution)/shard_map/ppermute | solution.py:14
  163.7 8.6 %copy-start.2 = (f32[2,256,256]{2,1,0:T(8,128)S(1)}, f32[2,256,256]{2,1,0:T(8,128)}, u32[]{:S(2)}) copy-start(f32[2,256,256]{2,1,0:T(8,128)} %param.13) | copy-start | bytes 1572868
  165.1 7.1 %collective-permute-start.1 = (f32[2,12288]{1,0:T(2,128)S(1)}, f32[2,12288]{1,0:T(2,128)S(1)}, u32[]{:S(2)}, u32[]{:S(2)}) collective-permute-start(f32[2,12288]{1,0:T(2,128)S(1)} %bitcast.66), channel_id=1, source_target_pairs={{0,8},{8,16},{16,24},{24,32},{32,40},{40,48},{48,56},{56,64},{64,7... | collective-permute-start | bytes 294920 | tf_op jit(solution)/shard_map/ppermute | solution.py:14
  167.3 5.1 %copy-start.4 = (f32[2,4]{1,0:T(2,128)S(1)}, f32[2,4]{1,0:T(2,128)}, u32[]{:S(2)}) copy-start(f32[2,4]{1,0:T(2,128)} %param.19) | copy-start | bytes 100
  172.4 3.3 %copy-start.1 = (f32[2,256,256]{2,1,0:T(8,128)}, f32[2,256,256]{2,1,0:T(8,128)S(1)}, u32[]{:S(2)}) copy-start(f32[2,256,256]{2,1,0:T(8,128)S(1)} %slice_subtract_fusion) | copy-start | bytes 1572868
Sparse Core Ops, SparseCore 0:
  175.8 28.5 reduce-scatter.1
where the time goes:
time: 212 us; the launch traced here: 211 us
  waiting for transfers between devices  88.6 us (42%)
  local copies, waits for them, and re-layouts  40.9 us (19%)
  starting transfers between devices  36 us (17%)
  matrix products  25.6 us (12%)
  between operations  14.3 us (7%)
  other arithmetic  5.06 us (2%)
    all_to_all x1, waiting for transfers between devices, per_device(): lax.all_to_all(send, ('ty', 'tx'), split_axis=0, concat_axis=0, tiled=True)  52.5 us
    reduce_scatter x1, waiting for transfers between devices, per_device(): lax.psum_scatter(jnp.einsum('bt,byx->tyx', fit_weight, residual, precisio...  28.8 us
    dot_general x16, matrix products, step(): jnp.einsum('hk,bkw->bhw', row_table, placed, preferred_element_type=jnp.f...  20.4 us
    all_to_all x1, starting transfers between devices, per_device(): lax.all_to_all(offs_send, ('ty', 'tx'), split_axis=0, concat_axis=0, tile...  17.3 us
    dynamic_slice x32, local copies, waits for them, and re-layouts, getter(): lax.dynamic_slice_in_dim(got, first, 16, 0)  16.5 us
    all_to_all x1, starting transfers between devices, per_device(): lax.all_to_all(send, ('ty', 'tx'), split_axis=0, concat_axis=0, tiled=True)  13.4 us
    reshape x16, local copies, waits for them, and re-layouts, step(): patch_four = patch_blk.reshape(block, bands_here, PATCH, PATCH)  8.83 us
    ppermute x2, waiting for transfers between devices, passed_along(): lax.ppermute(value, axis, [(source, source + steps) for source in range(i...  6.99 us
  transfers between devices with their start and end apart: 5, of which 5 were waited for; matrix products, arithmetic and copies ran while one was open for 4% of the time, Pallas kernels for 0%

commit v1 on v0

v1 whole, which is shorter than its diff:
```python
import functools

import jax
import jax.numpy as jnp
from jax import lax
from jax.experimental import pallas as pl
from jax.experimental.pallas import tpu as pltpu
from jax.sharding import PartitionSpec as P

TAYLOR = 4
SCALES = 5
PATCH = 48
ROWS_K = TAYLOR * SCALES
PAD_K = 24
HALF = PATCH // 2
WIDE = HALF * PATCH
SIDE = 256
SLOTS = 8
WORDS = 8
ROW_BASE = 48
COL_BASE = 64
BLOCKS = 6
CANVAS = 352
GROUP = 8
MESH = pl.DeviceIdType.MESH


def sends_of_tiles(tile, off, scale, amp, n_ty, n_tx):
    count = tile.shape[1]
    tiles, n_yp = n_ty * n_tx, n_ty // 2
    comp_y = lax.shift_right_logical(tile, n_tx.bit_length() - 1)
    comp_x = lax.bitwise_and(tile, n_tx - 1)
    over_r = (off[0:1] + PATCH > SIDE).astype(jnp.int32)
    over_c = (off[1:2] + PATCH > SIDE).astype(jnp.int32)
    dest = lax.broadcasted_iota(jnp.int32, (tiles, count), 0)
    half = tiles // 2
    bits = n_yp.bit_length() - 1
    core = lax.shift_right_logical(dest, half.bit_length() - 1)
    inner = lax.bitwise_and(dest, half - 1)
    dest_x = lax.shift_right_logical(inner, bits)
    dest_y = 2 * lax.bitwise_and(inner, n_yp - 1) + core
    down, right = dest_y - comp_y, dest_x - comp_x
    touches = ((down == 0) | ((down == 1) & (over_r == 1))) & (
        (right == 0) | ((right == 1) & (over_c == 1))
    )
    before = (
        lax.broadcasted_iota(jnp.int32, (count, count), 0)
        < lax.broadcasted_iota(jnp.int32, (count, count), 1)
    ).astype(jnp.float32)
    rank = jnp.dot(
        jnp.where(touches, 1.0, 0.0).astype(jnp.bfloat16),
        before.astype(jnp.bfloat16),
        preferred_element_type=jnp.float32,
    )
    rank = jnp.where(touches, rank, -1.0)
    chosen = jnp.concatenate(
        [jnp.where(rank == float(k), 1.0, 0.0).astype(jnp.bfloat16) for k in range(SLOTS)], axis=1
    )
    rows = (comp_y * SIDE + off[0:1]).astype(jnp.float32)
    cols = (comp_x * SIDE + off[1:2]).astype(jnp.float32)
    record = jnp.concatenate(
        [rows, cols, scale.astype(jnp.float32), jnp.ones((1, count), jnp.float32), amp], axis=0
    )
    high = record.astype(jnp.bfloat16).astype(jnp.float32)
    rest = record - high
    middle = rest.astype(jnp.bfloat16).astype(jnp.float32)
    low = rest - middle
    place = lax.shift_right_logical(
        lax.broadcasted_iota(jnp.int32, (SLOTS * WORDS, count), 0), 3
    )
    parts = []
    for part in (high, middle, low):
        tall = jnp.concatenate([part] * SLOTS, axis=0)
        parts.append(
            jnp.concatenate([jnp.where(place == k, tall, 0.0) for k in range(SLOTS)], axis=1)
        )
    parts.append(jnp.zeros_like(parts[0]))
    table = jnp.concatenate(parts, axis=0).astype(jnp.bfloat16)
    found = lax.dot_general(
        chosen, table, (((1,), (1,)), ((), ())), preferred_element_type=jnp.float32
    )
    found = found[:, :128] + found[:, 128:]
    found = found + pltpu.roll(found, 64, 1)
    lane = lax.broadcasted_iota(jnp.int32, (half, 128), 1)
    return jnp.where(lane < 64, found[:half], found[half:])


def unrolled(first, last, lane, step):
    tile, shift = divmod(step * PATCH, 128)
    out = []
    for table, base in ((first, 0), (last, 64)):
        value = table(tile)
        if shift + PATCH > 128:
            value = jnp.where(lane >= shift, value, table(tile + 1))
        turn = (base - shift) % 128
        out.append(pltpu.roll(value, turn, 1) if turn else value)
    return jnp.where(
        lane < PATCH, out[0], jnp.where((lane >= 64) & (lane < 64 + PATCH), out[1], 0.0)
    )


def exchange_kernel(
    n_band, n_ty, n_tx,
    tile_ref, off_ref, scale_ref, amp_ref, weight_ref, dirty_ref, psf_ref,
    place_ref, value_ref, list_ref, table_ref, taylor_table_ref, fit_ref,
    send, cross, got, psf, fit_send, fit_got, tab_send, tab_own, tab_got,
    x_send, x_recv, y_send, y_recv, b_send, b_recv, own_sem, pair_send, pair_recv,
):
    me_b, me_y, me_x = lax.axis_index("band"), lax.axis_index("ty"), lax.axis_index("tx")
    barrier = pltpu.get_barrier_semaphore()
    along_x = [lax.rem(me_x + o, n_tx) for o in range(1, n_tx)]
    along_y = [lax.rem(me_y + o, n_ty) for o in range(1, n_ty)]
    along_b = [lax.rem(me_b + o, n_band) for o in range(1, n_band)]
    partners = (
        [(me_b, me_y, x) for x in along_x]
        + [(me_b, y, me_x) for y in along_y]
        + [(b, me_y, me_x) for b in along_b]
    )
    for partner in partners:
        pl.semaphore_signal(barrier, inc=1, device_id=partner, device_id_type=MESH)

    records = sends_of_tiles(tile_ref[...], off_ref[...], scale_ref[...], amp_ref[...], n_ty, n_tx)
    n_yp = n_ty // 2
    for x in range(n_tx):
        send[x] = records[x * n_yp:(x + 1) * n_yp]

    for b in range(2):
        psf[b, 0:ROWS_K, :] = psf_ref[:, b, :].astype(jnp.float32)
        psf[b, ROWS_K:PAD_K, :] = jnp.zeros((PAD_K - ROWS_K, 2 * WIDE), jnp.float32)
    core = lax.rem(me_y, 2)
    mine = [
        jnp.where(core == 1, psf[b, :, WIDE:2 * WIDE], psf[b, :, 0:WIDE]) for b in range(2)
    ]
    for o in range(1, n_band):
        w0, w1 = weight_ref[0, along_b[o - 1]], weight_ref[1, along_b[o - 1]]
        tab_send[o - 1] = w0 * mine[0] + w1 * mine[1]
        fit_send[o - 1] = (w0 * dirty_ref[0] + w1 * dirty_ref[1]).astype(jnp.bfloat16)

    pl.semaphore_wait(barrier, len(partners))

    stage_x = []
    for o, x in enumerate(along_x):
        copy = pltpu.make_async_remote_copy(
            src_ref=send.at[x], dst_ref=cross.at[:, me_x, :],
            send_sem=x_send.at[o], recv_sem=x_recv.at[o],
            device_id=(me_b, me_y, x), device_id_type=MESH,
        )
        copy.start()
        stage_x.append(copy)
    own = pltpu.make_async_copy(send.at[me_x], cross.at[:, me_x, :], own_sem.at[0])
    own.start()
    stage_t, stage_f = [], []
    for source, target, which, copies in (
        (tab_send, tab_got, 0, stage_t), (fit_send, fit_got, 1, stage_f)
    ):
        for o, b in enumerate(along_b):
            copy = pltpu.make_async_remote_copy(
                src_ref=source.at[o], dst_ref=target.at[o],
                send_sem=b_send.at[which, o], recv_sem=b_recv.at[which, o],
                device_id=(b, me_y, me_x), device_id_type=MESH,
            )
            copy.start()
            copies.append(copy)

    w0, w1 = weight_ref[0, me_b], weight_ref[1, me_b]
    tab_own[core] = w0 * mine[0] + w1 * mine[1]
    lane24 = lax.broadcasted_iota(jnp.int32, (PAD_K, 128), 1)

    def piece(ref, half):
        return lambda t: ref[:, half * WIDE + t * 128:half * WIDE + (t + 1) * 128]

    def band_table(half):
        first, last = piece(psf.at[0], half), piece(psf.at[1], half)
        for step in range(HALF):
            table_ref[pl.ds(half * HALF + step, PAD_K, stride=PATCH), :] = unrolled(
                first, last, lane24, step
            )

    band_table(0)

    own.wait()
    for copy in stage_x:
        copy.wait_recv()
    stage_y = []
    for o, y in enumerate(along_y):
        copy = pltpu.make_async_remote_copy(
            src_ref=cross.at[y // 2], dst_ref=got.at[me_y],
            send_sem=y_send.at[o], recv_sem=y_recv.at[o],
            device_id=(me_b, y, me_x), device_id_type=MESH,
        )
        copy.start()
        stage_y.append(copy)
    own = pltpu.make_async_copy(cross.at[me_y // 2], got.at[me_y], own_sem.at[1])
    own.start()

    for copy in stage_t:
        copy.wait_recv()
    for o in range(n_band - 1):
        tab_own[core] += tab_got[o]
    band_table(1)
    pair = pltpu.make_async_remote_copy(
        src_ref=tab_own.at[core], dst_ref=tab_own.at[core],
        send_sem=pair_send.at[0], recv_sem=pair_recv.at[0],
        device_id=(me_b, me_y + 1 - 2 * core, me_x), device_id_type=MESH,
    )
    pair.start()

    own.wait()
    for copy in stage_y:
        copy.wait_recv()
    sources = n_ty * n_tx
    slots = jnp.concatenate([got[y] for y in range(n_ty)], axis=0)
    slots = jnp.where(lax.rem(me_y, 2) == 1, pltpu.roll(slots, 64, 1), slots)
    lane = lax.broadcasted_iota(jnp.int32, (sources, 128), 1)
    word = lax.bitwise_and(lane, WORDS - 1)
    move_r = (ROW_BASE - me_y * SIDE).astype(jnp.float32)
    move_c = (COL_BASE - me_x * SIDE).astype(jnp.float32)
    row = jnp.clip(slots + move_r, 0.0, float(ROW_BASE + SIDE)).astype(jnp.int32)
    col = jnp.clip(
        pltpu.roll(slots, 127, 1) + move_c, 0.0, float(COL_BASE + SIDE)
    ).astype(jnp.int32)
    scale = jnp.clip(pltpu.roll(slots, 126, 1), 0.0, float(SCALES)).astype(jnp.int32)
    place = row + lax.shift_right_logical(col, 6) * CANVAS
    place = place + lax.shift_left(lax.bitwise_and(col, 63), 12) + scale * (HALF << 18)
    lower = lax.broadcasted_iota(jnp.int32, (sources // 2, 128), 1) < 64
    for ref, value in ((place_ref, place), (value_ref, slots)):
        ref[0:sources // 2] = jnp.where(
            lower, value[:sources // 2], pltpu.roll(value[sources // 2:], 64, 1)
        )
        ref[sources // 2:sources // 2 + 8] = jnp.zeros((8, 128), ref.dtype)
    used = jnp.sum(
        jnp.where((word == 3) & (lane < 64), slots, 0.0), axis=1, keepdims=True
    )
    used = jnp.broadcast_to(used, (sources, 128))
    earlier = (
        lax.broadcasted_iota(jnp.int32, (sources, sources), 1)
        < lax.broadcasted_iota(jnp.int32, (sources, sources), 0)
    ).astype(jnp.float32).astype(jnp.bfloat16)
    start = jnp.dot(earlier, used.astype(jnp.bfloat16), preferred_element_type=jnp.float32)
    end = start + used
    lists = max(1, sources * SLOTS // 128)
    for i in range(lists):
        order = (lane + i * 128).astype(jnp.float32)
        source = jnp.sum(jnp.where(end <= order, 1.0, 0.0), axis=0, keepdims=True)
        base = jnp.max(jnp.where(start <= order, start, 0.0), axis=0, keepdims=True)
        upper = jnp.where(source >= float(sources // 2), 1.0, 0.0)
        index = (source - upper * (sources // 2)) * 128.0 + upper * 64.0
        index = index + (order[0:1] - base) * WORDS
        index = jnp.where(source < float(sources), index, float(sources // 2 * 128))
        list_ref[i:i + 1, :] = index.astype(jnp.int32)
    list_ref[lists:lists + 1, :] = end[sources - 1:sources].astype(jnp.int32)

    pair.wait_recv()
    first, last = piece(tab_own.at[0], 0), piece(tab_own.at[1], 0)
    for step in range(HALF):
        taylor_table_ref[pl.ds(step, PAD_K, stride=HALF), :] = unrolled(first, last, lane24, step)

    fit_ref[...] = w0 * dirty_ref[0] + w1 * dirty_ref[1]
    for copy in stage_f:
        copy.wait_recv()
    for o in range(n_band - 1):
        fit_ref[...] += fit_got[o].astype(jnp.float32)
    for copy in stage_x + stage_y + stage_t + stage_f + [pair]:
        copy.wait_send()


def render_kernel(
    place_ref, amp_ref, list_ref, table_ref, taylor_table_ref, dirty_ref, fit_ref,
    residual_ref, taylor_ref, canvas, spill, canvas_t, spill_t,
):
    for block in range(BLOCKS - 1):
        for ref, used, first in (
            (canvas, block > 0, ROW_BASE), (spill, block < 4, ROW_BASE),
            (canvas_t, block > 0, ROW_BASE - HALF), (spill_t, block < 4, ROW_BASE - HALF),
        ):
            if used:
                rows = ROW_BASE + SIDE - first
                ref[pl.ds(block * CANVAS + first, rows), :] = jnp.zeros((rows, 128), jnp.float32)
    half_lane = lax.bitwise_and(lax.broadcasted_iota(jnp.int32, (HALF, 128), 1), 63)
    count = list_ref[list_ref.shape[0] - 1024]

    def step(index, carry):
        for g in range(GROUP):
            slot = list_ref[index * GROUP + g]
            packed = place_ref[slot]
            amps = [amp_ref[slot + 4 + t] for t in range(TAYLOR)]
            first = lax.bitwise_and(packed, 4095)
            shift = lax.bitwise_and(lax.shift_right_logical(packed, 12), 63)
            base = lax.shift_right_logical(packed, 18)
            low = pl.multiple_of(base, HALF)
            high = pl.multiple_of(2 * base, PATCH)
            patch = fit = None
            for t in range(TAYLOR):
                term = amps[t] * table_ref[pl.ds(high + t * SCALES * PATCH, PATCH), :]
                patch = term if t == 0 else patch + term
                term = amps[t] * taylor_table_ref[pl.ds(low + t * SCALES * HALF, HALF), :]
                fit = term if t == 0 else fit + term
            patch = patch.astype(jnp.bfloat16).astype(jnp.float32)
            keep = half_lane >= shift
            other = jnp.logical_not(keep)
            sums = []
            for value, inside, beyond, at in (
                (patch[:HALF], canvas, spill, first),
                (patch[HALF:], canvas, spill, first + HALF),
                (fit, canvas_t, spill_t, first),
            ):
                value = pltpu.roll(value, shift, 1)
                for mask, target in ((keep, inside), (other, beyond)):
                    here = target.at[pl.ds(at, HALF), :]
                    sums.append((here, here[...] + value, mask))
            for here, value, mask in sums:
                pltpu.store(here, value, mask=mask)
        return carry

    lax.fori_loop(0, (count + GROUP - 1) // GROUP, step, 0)

    rows = 64
    lower = lax.broadcasted_iota(jnp.int32, (rows, 128), 1) < 64

    def mix(low, high):
        return jnp.where(lower, low, high)

    for r in range(0, SIDE, rows):
        for j in range(2):

            def at(ref, block, first):
                start = (block + 2 * j) * CANVAS + ROW_BASE + r + first
                return ref[pl.ds(start, rows), :]

            c1, c2 = at(canvas, 1, 0), at(canvas, 2, 0)
            s1, s2 = at(spill, 0, 0), at(spill, 1, 0)
            here = (slice(r, r + rows), slice(j * 128, j * 128 + 128))
            model = mix(c1, s2) + pltpu.roll(mix(c2, s1), 64, 1)
            residual_ref[(0,) + here] = dirty_ref[(0,) + here] - model
            model = mix(s1, c2) + pltpu.roll(mix(s2, c1), 64, 1)
            residual_ref[(1,) + here] = dirty_ref[(1,) + here] - model
            straight = mix(
                at(canvas_t, 1, 0) + at(spill_t, 0, -HALF), at(canvas_t, 2, -HALF) + at(spill_t, 1, 0)
            )
            crossed = mix(
                at(canvas_t, 2, 0) + at(spill_t, 1, -HALF), at(canvas_t, 1, -HALF) + at(spill_t, 0, 0)
            )
            taylor_ref[here] = fit_ref[here] - (straight + pltpu.roll(crossed, 64, 1))


def per_device(dirty, psf, comp_tile, comp_offset, comp_scale, comp_amp, fit_weight):
    n_band, n_ty, n_tx = (lax.axis_size(a) for a in ("band", "ty", "tx"))
    sources = n_ty * n_tx
    lists = max(1, sources * SLOTS // 128)
    n_yp = n_ty // 2
    vmem = pl.BlockSpec(memory_space=pltpu.VMEM)
    smem = pl.BlockSpec(memory_space=pltpu.SMEM)
    dma = pltpu.SemaphoreType.DMA
    f32, bf16 = jnp.float32, jnp.bfloat16
    place, value, order, table, taylor_table, fit = pl.pallas_call(
        functools.partial(exchange_kernel, n_band, n_ty, n_tx),
        out_shape=(
            jax.ShapeDtypeStruct((sources // 2 + 8, 128), jnp.int32),
            jax.ShapeDtypeStruct((sources // 2 + 8, 128), f32),
            jax.ShapeDtypeStruct((lists + 8, 128), jnp.int32),
            jax.ShapeDtypeStruct((PAD_K * PATCH, 128), f32),
            jax.ShapeDtypeStruct((PAD_K * HALF, 128), f32),
            jax.ShapeDtypeStruct((SIDE, SIDE), f32),
        ),
        in_specs=[vmem] * 4 + [smem] + [vmem] * 2,
        out_specs=(vmem,) * 6,
        scratch_shapes=[
            pltpu.VMEM((n_tx, n_yp, 128), f32),
            pltpu.VMEM((n_yp, n_tx, 128), f32),
            pltpu.VMEM((n_ty, n_tx, 128), f32),
            pltpu.VMEM((2, PAD_K, 2 * WIDE), f32),
            pltpu.VMEM((n_band - 1, SIDE, SIDE), bf16),
            pltpu.VMEM((n_band - 1, SIDE, SIDE), bf16),
            pltpu.VMEM((n_band - 1, PAD_K, WIDE), f32),
            pltpu.VMEM((2, PAD_K, WIDE), f32),
            pltpu.VMEM((n_band - 1, PAD_K, WIDE), f32),
            dma((n_tx - 1,)), dma((n_tx - 1,)),
            dma((n_ty - 1,)), dma((n_ty - 1,)),
            dma((2, n_band - 1)), dma((2, n_band - 1)),
            dma((2,)), dma((1,)), dma((1,)),
        ],
        compiler_params=pltpu.CompilerParams(
            collective_id=0, has_side_effects=True, vmem_limit_bytes=24 * 1024 * 1024
        ),
    )(
        comp_tile.T, comp_offset.T, comp_scale[None, :], comp_amp.T, fit_weight, dirty,
        psf.transpose(1, 0, 2),
    )
    residual, taylor = pl.pallas_call(
        render_kernel,
        out_shape=(
            jax.ShapeDtypeStruct((2, SIDE, SIDE), f32),
            jax.ShapeDtypeStruct((SIDE, SIDE), f32),
        ),
        in_specs=[smem] * 3 + [vmem] * 4,
        out_specs=(vmem,) * 2,
        scratch_shapes=[
            pltpu.VMEM(((BLOCKS - 1) * CANVAS, 128), f32) for _ in range(4)
        ],
        compiler_params=pltpu.CompilerParams(vmem_limit_bytes=24 * 1024 * 1024),
    )(
        place.reshape(-1), value.reshape(-1), order.reshape(-1), table, taylor_table, dirty, fit,
    )
    return residual, taylor[None]


def solution(mesh):
    return jax.shard_map(
        per_device,
        mesh=mesh,
        in_specs=(
            P("band", "ty", "tx"),
            P("band", None, None),
            P(("ty", "tx"), None),
            P(("ty", "tx"), None),
            P(("ty", "tx")),
            P(("ty", "tx"), None),
            P("band", None),
        ),
        out_specs=(P("band", "ty", "tx"), P("band", "ty", "tx")),
        check_vma=False,
    )
```

time: 212 us -> 37 us (0.17)
  the two profiles are of different devices: /device:TPU:32 before, /device:TPU:88 now
where the time goes in v1:
time: 37 us; the launch traced here: 36.6 us
  Pallas kernels  33.2 us (90%)
  local copies, waits for them, and re-layouts  2.66 us (7%)
  between operations  0.69 us (2%)
    pallas_call x1, Pallas kernels, per_device(): pl.pallas_call(functools.partial(exchange_kernel, n_band, n_ty, n_tx), ou...  24 us
    pallas_call x1, Pallas kernels, per_device(): pl.pallas_call(render_kernel, out_shape=(jax.ShapeDtypeStruct((2, SIDE, S...  9.18 us
    unnamed x16, local copies, waits for them, and re-layouts  2.66 us

profile of v1, /device:TPU:88, one launch (start us, length us, event | category | flops | bytes accessed | tf_op | source)
XLA Modules:
  0.0 36.6 jit_solution(1667833825881865867)
XLA Ops:
  0.6 0.0 copy-start.5
  0.6 0.0 copy-start.7
  0.7 0.0 copy-start.3
  0.7 0.0 copy-start.4
  0.7 0.0 copy-start.6
  0.7 0.6 %copy-done.5 = f32[2,4]{1,0:T(2,128)S(1)} copy-done((f32[2,4]{1,0:T(2,128)S(1)}, f32[2,4]{1,0:T(2,128)}, u32[]{:S(2)}) %copy-start.5) | copy-done | bytes 56
  1.3 0.0 copy-done.7
  1.3 0.0 copy-done.3
  1.3 0.0 copy-done.4
  1.4 0.0 copy-done.6
  1.4 0.0 copy-start
  1.4 1.0 %copy-done = f32[2,256,256]{2,1,0:T(8,128)S(1)} copy-done((f32[2,256,256]{2,1,0:T(8,128)S(1)}, f32[2,256,256]{2,1,0:T(8,128)}, u32[]{:S(2)}) %copy-start) | copy-done | bytes 524312
  2.4 0.0 copy-start.2
  2.4 0.9 %copy-done.2 = bf16[2,20,2304]{2,0,1:T(2,128)(2,1)S(1)} copy-done((bf16[2,20,2304]{2,0,1:T(2,128)(2,1)S(1)}, bf16[2,20,2304]{2,0,1:T(2,128)(2,1)}, u32[]{:S(2)}) %copy-start.2) | copy-done | bytes 184344
  3.3 0.0 copy-start.1
  3.3 24.0 %shard_map.86 = (s32[72,128]{1,0:T(8,128)S(1)}, f32[72,128]{1,0:T(8,128)S(1)}, s32[16,128]{1,0:T(8,128)S(1)}, f32[1152,128]{1,0:T(8,128)S(1)}, f32[576,128]{1,0:T(8,128)S(1)}, /*index=5*/f32[256,256]{1,0:T(8,128)S(1)}) custom-call(s32[1,128]{1,0:T(1,128)S(1)} %bitcast.15, s32[2,128]{1,0:T(2,128)S(1)} %bitcast.14, s32[1,128]{1,0:T(1,128)S(1)} %bitcast.16, ...), custom_call_target="tpu_custom_call" | custom-call | tf_op jit(solution)/shard_map/pallas_call | solution.py:355
  27.4 0.0 copy-done.1
  27.4 9.2 %shard_map.87 = (f32[2,256,256]{2,1,0:T(8,128)}, f32[256,256]{1,0:T(8,128)}) custom-call(s32[9216]{0:T(1024)S(1)} %bitcast.10, f32[9216]{0:T(1024)S(1)} %bitcast.11, s32[2048]{0:T(1024)S(1)} %bitcast.12, f32[1152,128]{1,0:T(8,128)S(1)} %get-tuple-element.13.table_ref, f32[576,128]{1,0:T(8,128)S(1)} %get-tuple-element.14.taylor_table_ref, ...), custom_call_target="tpu_custom_call" | custom-call | tf_op jit(solution)/shard_map/pallas_call | solution.py:389
Async XLA Ops:
  0.6 0.7 %copy-start.5 = (f32[2,4]{1,0:T(2,128)S(1)}, f32[2,4]{1,0:T(2,128)}, u32[]{:S(2)}) copy-start(f32[2,4]{1,0:T(2,128)} %weight_ref.1) | copy-start | bytes 100
  0.6 0.7 %copy-start.7 = (s32[128]{0:T(128)S(1)}, s32[128]{0:T(128)}, u32[]{:S(2)}) copy-start(s32[128]{0:T(128)} %param.11) | copy-start | bytes 1540
  0.7 0.7 %copy-start.3 = (f32[128,4]{0,1:T(4,128)S(1)}, f32[128,4]{0,1:T(4,128)}, u32[]{:S(2)}) copy-start(f32[128,4]{0,1:T(4,128)} %param.12) | copy-start | bytes 6148
  0.7 0.7 %copy-start.4 = (s32[128,2]{0,1:T(2,128)S(1)}, s32[128,2]{0,1:T(2,128)}, u32[]{:S(2)}) copy-start(s32[128,2]{0,1:T(2,128)} %param.10) | copy-start | bytes 3076
  0.7 0.7 %copy-start.6 = (s32[128,1]{0,1:T(1,128)S(1)}, s32[128,1]{0,1:T(1,128)}, u32[]{:S(2)}) copy-start(s32[128,1]{0,1:T(1,128)} %param.9) | copy-start | bytes 1540
  1.4 1.0 %copy-start = (f32[2,256,256]{2,1,0:T(8,128)S(1)}, f32[2,256,256]{2,1,0:T(8,128)}, u32[]{:S(2)}) copy-start(f32[2,256,256]{2,1,0:T(8,128)} %dirty_ref.3) | copy-start | bytes 1572868
  2.4 0.9 %copy-start.2 = (bf16[2,20,2304]{2,0,1:T(2,128)(2,1)S(1)}, bf16[2,20,2304]{2,0,1:T(2,128)(2,1)}, u32[]{:S(2)}) copy-start(bf16[2,20,2304]{2,0,1:T(2,128)(2,1)} %param.8) | copy-start | bytes 552964
  3.3 24.0 %copy-start.1 = (f32[2,256,256]{2,1,0:T(8,128)S(1)}, f32[2,256,256]{2,1,0:T(8,128)}, u32[]{:S(2)}) copy-start(f32[2,256,256]{2,1,0:T(8,128)} %dirty_ref.3) | copy-start | bytes 1572868

commit v2 on v1

--- a/solution.py
+++ b/solution.py
@@ -101,11 +101,17 @@
 
 def exchange_kernel(
     n_band, n_ty, n_tx,
-    tile_ref, off_ref, scale_ref, amp_ref, weight_ref, dirty_ref, psf_ref,
-    place_ref, value_ref, list_ref, table_ref, taylor_table_ref, fit_ref,
-    send, cross, got, psf, fit_send, fit_got, tab_send, tab_own, tab_got,
-    x_send, x_recv, y_send, y_recv, b_send, b_recv, own_sem, pair_send, pair_recv,
+    tile_ref, off_ref, scale_ref, amp_ref, weight_ref, dirty_hbm, psf_hbm,
+    value_ref, list_ref, table_ref, taylor_table_ref, fit_ref,
+    send, cross, got, dirty_ref, psf_ref, psf, fit_send, fit_got, tab_send, tab_own, tab_got,
+    x_send, x_recv, y_send, y_recv, b_send, b_recv, own_sem, pair_send, pair_recv, load_sem,
 ):
+    loads = [
+        pltpu.make_async_copy(psf_hbm, psf_ref, load_sem.at[0]),
+        pltpu.make_async_copy(dirty_hbm, dirty_ref, load_sem.at[1]),
+    ]
+    for load in loads:
+        load.start()
     me_b, me_y, me_x = lax.axis_index("band"), lax.axis_index("ty"), lax.axis_index("tx")
     barrier = pltpu.get_barrier_semaphore()
     along_x = [lax.rem(me_x + o, n_tx) for o in range(1, n_tx)]
@@ -124,6 +130,21 @@
     for x in range(n_tx):
         send[x] = records[x * n_yp:(x + 1) * n_yp]
 
+    pl.semaphore_wait(barrier, len(partners))
+
+    stage_x = []
+    for o, x in enumerate(along_x):
+        copy = pltpu.make_async_remote_copy(
+            src_ref=send.at[x], dst_ref=cross.at[:, me_x, :],
+            send_sem=x_send.at[o], recv_sem=x_recv.at[o],
+            device_id=(me_b, me_y, x), device_id_type=MESH,
+        )
+        copy.start()
+        stage_x.append(copy)
+    own = pltpu.make_async_copy(send.at[me_x], cross.at[:, me_x, :], own_sem.at[0])
+    own.start()
+    for load in loads:
+        load.wait()
     for b in range(2):
         psf[b, 0:ROWS_K, :] = psf_ref[:, b, :].astype(jnp.float32)
         psf[b, ROWS_K:PAD_K, :] = jnp.zeros((PAD_K - ROWS_K, 2 * WIDE), jnp.float32)
@@ -136,19 +157,22 @@
         tab_send[o - 1] = w0 * mine[0] + w1 * mine[1]
         fit_send[o - 1] = (w0 * dirty_ref[0] + w1 * dirty_ref[1]).astype(jnp.bfloat16)
 
-    pl.semaphore_wait(barrier, len(partners))
-
-    stage_x = []
-    for o, x in enumerate(along_x):
-        copy = pltpu.make_async_remote_copy(
-            src_ref=send.at[x], dst_ref=cross.at[:, me_x, :],
-            send_sem=x_send.at[o], recv_sem=x_recv.at[o],
-            device_id=(me_b, me_y, x), device_id_type=MESH,
-        )
-        copy.start()
-        stage_x.append(copy)
-    own = pltpu.make_async_copy(send.at[me_x], cross.at[:, me_x, :], own_sem.at[0])
-    own.start()
+    w0, w1 = weight_ref[0, me_b], weight_ref[1, me_b]
+    tab_own[core] = w0 * mine[0] + w1 * mine[1]
+    lane24 = lax.broadcasted_iota(jnp.int32, (PAD_K, 128), 1)
+
+    def piece(ref, half):
+        return lambda t: ref[:, half * WIDE + t * 128:half * WIDE + (t + 1) * 128]
+
+    def band_table(half):
+        first, last = piece(psf.at[0], half), piece(psf.at[1], half)
+        for step in range(HALF):
+            table_ref[pl.ds(half * HALF + step, PAD_K, stride=PATCH), :] = unrolled(
+                first, last, lane24, step
+            )
+
+    band_table(0)
+
     stage_t, stage_f = [], []
     for source, target, which, copies in (
         (tab_send, tab_got, 0, stage_t), (fit_send, fit_got, 1, stage_f)
@@ -161,22 +185,6 @@
             )
             copy.start()
             copies.append(copy)
-
-    w0, w1 = weight_ref[0, me_b], weight_ref[1, me_b]
-    tab_own[core] = w0 * mine[0] + w1 * mine[1]
-    lane24 = lax.broadcasted_iota(jnp.int32, (PAD_K, 128), 1)
-
-    def piece(ref, half):
-        return lambda t: ref[:, half * WIDE + t * 128:half * WIDE + (t + 1) * 128]
-
-    def band_table(half):
-        first, last = piece(psf.at[0], half), piece(psf.at[1], half)
-        for step in range(HALF):
-            table_ref[pl.ds(half * HALF + step, PAD_K, stride=PATCH), :] = unrolled(
-                first, last, lane24, step
-            )
-
-    band_table(0)
 
     own.wait()
     for copy in stage_x:
@@ -221,13 +229,13 @@
     ).astype(jnp.int32)
     scale = jnp.clip(pltpu.roll(slots, 126, 1), 0.0, float(SCALES)).astype(jnp.int32)
     place = row + lax.shift_right_logical(col, 6) * CANVAS
-    place = place + lax.shift_left(lax.bitwise_and(col, 63), 12) + scale * (HALF << 18)
+    place = place + lax.shift_left(lax.bitwise_and(col, 63), 11) + lax.shift_left(scale, 17)
+    value = jnp.where(word == 0, place.astype(jnp.float32), slots)
     lower = lax.broadcasted_iota(jnp.int32, (sources // 2, 128), 1) < 64
-    for ref, value in ((place_ref, place), (value_ref, slots)):
-        ref[0:sources // 2] = jnp.where(
-            lower, value[:sources // 2], pltpu.roll(value[sources // 2:], 64, 1)
-        )
-        ref[sources // 2:sources // 2 + 8] = jnp.zeros((8, 128), ref.dtype)
+    value_ref[0:sources // 2] = jnp.where(
+        lower, value[:sources // 2], pltpu.roll(value[sources // 2:], 64, 1)
+    )
+    value_ref[sources // 2:sources // 2 + 8] = jnp.zeros((8, 128), jnp.float32)
     used = jnp.sum(
         jnp.where((word == 3) & (lane < 64), slots, 0.0), axis=1, keepdims=True
     )
@@ -265,9 +273,16 @@
 
 
 def render_kernel(
-    place_ref, amp_ref, list_ref, table_ref, taylor_table_ref, dirty_ref, fit_ref,
-    residual_ref, taylor_ref, canvas, spill, canvas_t, spill_t,
+    value_ref, order_ref, table_ref, taylor_table_ref, dirty_ref, fit_ref,
+    residual_hbm, taylor_hbm,
+    canvas, spill, canvas_t, spill_t, residual_ref, taylor_ref, amp_ref, list_ref, sems, out_sems,
 ):
+    fetches = [
+        pltpu.make_async_copy(value_ref, amp_ref, sems.at[0]),
+        pltpu.make_async_copy(order_ref, list_ref, sems.at[1]),
+    ]
+    for fetch in fetches:
+        fetch.start()
     for block in range(BLOCKS - 1):
         for ref, used, first in (
             (canvas, block > 0, ROW_BASE), (spill, block < 4, ROW_BASE),
@@ -276,17 +291,19 @@
             if used:
                 rows = ROW_BASE + SIDE - first
                 ref[pl.ds(block * CANVAS + first, rows), :] = jnp.zeros((rows, 128), jnp.float32)
+    for fetch in fetches:
+        fetch.wait()
     half_lane = lax.bitwise_and(lax.broadcasted_iota(jnp.int32, (HALF, 128), 1), 63)
     count = list_ref[list_ref.shape[0] - 1024]
 
     def step(index, carry):
         for g in range(GROUP):
             slot = list_ref[index * GROUP + g]
-            packed = place_ref[slot]
+            packed = amp_ref[slot].astype(jnp.int32)
             amps = [amp_ref[slot + 4 + t] for t in range(TAYLOR)]
-            first = lax.bitwise_and(packed, 4095)
-            shift = lax.bitwise_and(lax.shift_right_logical(packed, 12), 63)
-            base = lax.shift_right_logical(packed, 18)
+            first = lax.bitwise_and(packed, 2047)
+            shift = lax.bitwise_and(lax.shift_right_logical(packed, 11), 63)
+            base = lax.shift_right_logical(packed, 17) * HALF
             low = pl.multiple_of(base, HALF)
             high = pl.multiple_of(2 * base, PATCH)
             patch = fit = None
@@ -320,6 +337,7 @@
     def mix(low, high):
         return jnp.where(lower, low, high)
 
+    copies = []
     for r in range(0, SIDE, rows):
         for j in range(2):
 
@@ -341,6 +359,23 @@
                 at(canvas_t, 2, 0) + at(spill_t, 1, -HALF), at(canvas_t, 1, -HALF) + at(spill_t, 0, 0)
             )
             taylor_ref[here] = fit_ref[here] - (straight + pltpu.roll(crossed, 64, 1))
+        part = r // rows
+        copies.append(
+            pltpu.make_async_copy(
+                residual_ref.at[:, pl.ds(r, rows), :], residual_hbm.at[:, pl.ds(r, rows), :],
+                out_sems.at[0, part],
+            )
+        )
+        copies.append(
+            pltpu.make_async_copy(
+                taylor_ref.at[pl.ds(r, rows), :], taylor_hbm.at[pl.ds(r, rows), :],
+                out_sems.at[1, part],
+            )
+        )
+        copies[-2].start()
+        copies[-1].start()
+    for copy in copies:
+        copy.wait()
 
 
 def per_device(dirty, psf, comp_tile, comp_offset, comp_scale, comp_amp, fit_weight):
@@ -352,22 +387,23 @@
     smem = pl.BlockSpec(memory_space=pltpu.SMEM)
     dma = pltpu.SemaphoreType.DMA
     f32, bf16 = jnp.float32, jnp.bfloat16
-    place, value, order, table, taylor_table, fit = pl.pallas_call(
+    value, order, table, taylor_table, fit = pl.pallas_call(
         functools.partial(exchange_kernel, n_band, n_ty, n_tx),
         out_shape=(
-            jax.ShapeDtypeStruct((sources // 2 + 8, 128), jnp.int32),
             jax.ShapeDtypeStruct((sources // 2 + 8, 128), f32),
             jax.ShapeDtypeStruct((lists + 8, 128), jnp.int32),
             jax.ShapeDtypeStruct((PAD_K * PATCH, 128), f32),
             jax.ShapeDtypeStruct((PAD_K * HALF, 128), f32),
             jax.ShapeDtypeStruct((SIDE, SIDE), f32),
         ),
-        in_specs=[vmem] * 4 + [smem] + [vmem] * 2,
-        out_specs=(vmem,) * 6,
+        in_specs=[vmem] * 4 + [smem] + [pl.BlockSpec(memory_space=pltpu.HBM)] * 2,
+        out_specs=(vmem,) * 5,
         scratch_shapes=[
             pltpu.VMEM((n_tx, n_yp, 128), f32),
             pltpu.VMEM((n_yp, n_tx, 128), f32),
             pltpu.VMEM((n_ty, n_tx, 128), f32),
+            pltpu.VMEM((2, SIDE, SIDE), f32),
+            pltpu.VMEM((ROWS_K, 2, 2 * WIDE), bf16),
             pltpu.VMEM((2, PAD_K, 2 * WIDE), f32),
             pltpu.VMEM((n_band - 1, SIDE, SIDE), bf16),
             pltpu.VMEM((n_band - 1, SIDE, SIDE), bf16),
@@ -377,14 +413,15 @@
             dma((n_tx - 1,)), dma((n_tx - 1,)),
             dma((n_ty - 1,)), dma((n_ty - 1,)),
             dma((2, n_band - 1)), dma((2, n_band - 1)),
-            dma((2,)), dma((1,)), dma((1,)),
+            dma((2,)), dma((1,)), dma((1,)), dma((2,)),
         ],
         compiler_params=pltpu.CompilerParams(
             collective_id=0, has_side_effects=True, vmem_limit_bytes=24 * 1024 * 1024
         ),
     )(
-        comp_tile.T, comp_offset.T, comp_scale[None, :], comp_amp.T, fit_weight, dirty,
-        psf.transpose(1, 0, 2),
+        comp_tile.T, comp_offset.T, comp_scale[None, :], comp_amp.T, fit_weight,
+        pltpu.with_memory_space_constraint(dirty, pltpu.HBM),
+        pltpu.with_memory_space_constraint(psf.transpose(1, 0, 2), pltpu.HBM),
     )
     residual, taylor = pl.pallas_call(
         render_kernel,
@@ -392,14 +429,18 @@
             jax.ShapeDtypeStruct((2, SIDE, SIDE), f32),
             jax.ShapeDtypeStruct((SIDE, SIDE), f32),
         ),
-        in_specs=[smem] * 3 + [vmem] * 4,
-        out_specs=(vmem,) * 2,
+        in_specs=[vmem] * 6,
+        out_specs=(pl.BlockSpec(memory_space=pltpu.HBM),) * 2,
         scratch_shapes=[
             pltpu.VMEM(((BLOCKS - 1) * CANVAS, 128), f32) for _ in range(4)
+        ] + [
+            pltpu.VMEM((2, SIDE, SIDE), f32), pltpu.VMEM((SIDE, SIDE), f32),
+            pltpu.SMEM((value.size,), f32), pltpu.SMEM((order.size,), jnp.int32),
+            dma((2,)), dma((2, SIDE // 64)),
         ],
         compiler_params=pltpu.CompilerParams(vmem_limit_bytes=24 * 1024 * 1024),
     )(
-        place.reshape(-1), value.reshape(-1), order.reshape(-1), table, taylor_table, dirty, fit,
+        value.reshape(-1), order.reshape(-1), table, taylor_table, dirty, fit,
     )
     return residual, taylor[None]
 

time: 37 us -> 37.1 us (level)
  the two profiles are of different devices: /device:TPU:88 before, /device:TPU:96 now
where the time goes in v2:
time: 37.1 us; the launch traced here: 37 us
  Pallas kernels  32.9 us (89%)
  local copies, waits for them, and re-layouts  3.4 us (9%)
  between operations  0.67 us (2%)
    pallas_call x1, Pallas kernels, per_device(): pl.pallas_call(functools.partial(exchange_kernel, n_band, n_ty, n_tx), ou...  24.4 us
    pallas_call x1, Pallas kernels, per_device(): pl.pallas_call(render_kernel, out_shape=(jax.ShapeDtypeStruct((2, SIDE, S...  8.49 us
    unnamed x12, local copies, waits for them, and re-layouts  3.4 us

profile of v2, /device:TPU:96, one launch (start us, length us, event | category | flops | bytes accessed | tf_op | source)
XLA Modules:
  0.0 37.0 jit_solution(5520879834279087408)
XLA Ops:
  0.6 0.0 copy-start
  0.6 0.0 copy-start.1
  0.7 0.7 %copy-done.1 = f32[128,4]{0,1:T(4,128)S(1)} copy-done((f32[128,4]{0,1:T(4,128)S(1)}, f32[128,4]{0,1:T(4,128)}, u32[]{:S(2)}) %copy-start.1) | copy-done | bytes 2072
  1.4 0.0 copy-start.2
  1.4 0.7 %copy-done.2 = s32[128,2]{0,1:T(2,128)S(1)} copy-done((s32[128,2]{0,1:T(2,128)S(1)}, s32[128,2]{0,1:T(2,128)}, u32[]{:S(2)}) %copy-start.2) | copy-done | bytes 1048
  2.1 0.0 copy-start.3
  2.1 0.7 %copy-done.3 = f32[2,4]{1,0:T(2,128)S(1)} copy-done((f32[2,4]{1,0:T(2,128)S(1)}, f32[2,4]{1,0:T(2,128)}, u32[]{:S(2)}) %copy-start.3) | copy-done | bytes 56
  2.7 0.0 copy-start.4
  2.7 0.7 %copy-done.4 = s32[128,1]{0,1:T(1,128)S(1)} copy-done((s32[128,1]{0,1:T(1,128)S(1)}, s32[128,1]{0,1:T(1,128)}, u32[]{:S(2)}) %copy-start.4) | copy-done | bytes 536
  3.4 0.0 copy-start.5
  3.4 0.7 %copy-done.5 = s32[128]{0:T(128)S(1)} copy-done((s32[128]{0:T(128)S(1)}, s32[128]{0:T(128)}, u32[]{:S(2)}) %copy-start.5) | copy-done | bytes 536
  4.1 24.4 %shard_map.86 = (f32[72,128]{1,0:T(8,128)S(1)}, s32[16,128]{1,0:T(8,128)S(1)}, f32[1152,128]{1,0:T(8,128)S(1)}, f32[576,128]{1,0:T(8,128)S(1)}, f32[256,256]{1,0:T(8,128)S(1)}) custom-call(s32[1,128]{1,0:T(1,128)S(1)} %bitcast.12, s32[2,128]{1,0:T(2,128)S(1)} %bitcast.11, s32[1,128]{1,0:T(1,128)S(1)} %bitcast.13, f32[4,128]{1,0:T(4,128)S(1)} %bitcast.10, ...), custom_call_target="tpu_custom_call" | custom-call | tf_op jit(solution)/shard_map/pallas_call | solution.py:390
  28.5 0.0 copy-done
  28.5 8.5 %shard_map.87 = (f32[2,256,256]{2,1,0:T(8,128)}, f32[256,256]{1,0:T(8,128)}) custom-call(f32[9216]{0:T(1024)S(1)} %bitcast.8, s32[2048]{0:T(1024)S(1)} %bitcast.9, f32[1152,128]{1,0:T(8,128)S(1)} %get-tuple-element.11.table_ref, f32[576,128]{1,0:T(8,128)S(1)} %get-tuple-element.12.taylor_table_ref, f32[2,256,256]{2,1,0:T(8,128)S(1)} %copy-done, ...), custom_call_target="tpu_custom_call" | custom-call | tf_op jit(solution)/shard_map/pallas_call | solution.py:426
Async XLA Ops:
  0.6 27.8 %copy-start = (f32[2,256,256]{2,1,0:T(8,128)S(1)}, f32[2,256,256]{2,1,0:T(8,128)}, u32[]{:S(2)}) copy-start(f32[2,256,256]{2,1,0:T(8,128)} %dirty_ref.1) | copy-start | bytes 1572868
  0.6 0.7 %copy-start.1 = (f32[128,4]{0,1:T(4,128)S(1)}, f32[128,4]{0,1:T(4,128)}, u32[]{:S(2)}) copy-start(f32[128,4]{0,1:T(4,128)} %param.12) | copy-start | bytes 6148
  1.4 0.7 %copy-start.2 = (s32[128,2]{0,1:T(2,128)S(1)}, s32[128,2]{0,1:T(2,128)}, u32[]{:S(2)}) copy-start(s32[128,2]{0,1:T(2,128)} %param.10) | copy-start | bytes 3076
  2.1 0.7 %copy-start.3 = (f32[2,4]{1,0:T(2,128)S(1)}, f32[2,4]{1,0:T(2,128)}, u32[]{:S(2)}) copy-start(f32[2,4]{1,0:T(2,128)} %weight_ref.1) | copy-start | bytes 100
  2.7 0.7 %copy-start.4 = (s32[128,1]{0,1:T(1,128)S(1)}, s32[128,1]{0,1:T(1,128)}, u32[]{:S(2)}) copy-start(s32[128,1]{0,1:T(1,128)} %param.9) | copy-start | bytes 1540
  3.4 0.7 %copy-start.5 = (s32[128]{0:T(128)S(1)}, s32[128]{0:T(128)}, u32[]{:S(2)}) copy-start(s32[128]{0:T(128)} %param.11) | copy-start | bytes 1540

commit v3 on v2

--- a/solution.py
+++ b/solution.py
@@ -101,14 +101,18 @@
 
 def exchange_kernel(
     n_band, n_ty, n_tx,
-    tile_ref, off_ref, scale_ref, amp_ref, weight_ref, dirty_hbm, psf_hbm,
+    tile_hbm, off_hbm, scale_hbm, amp_hbm, weight_hbm, dirty_hbm, psf_hbm,
     value_ref, list_ref, table_ref, taylor_table_ref, fit_ref,
-    send, cross, got, dirty_ref, psf_ref, psf, fit_send, fit_got, tab_send, tab_own, tab_got,
+    tile_ref, off_ref, scale_ref, amp_ref, weight_ref, dirty_ref, psf_ref,
+    send, cross, got, psf, fit_send, fit_got, tab_send, tab_own, tab_got,
     x_send, x_recv, y_send, y_recv, b_send, b_recv, own_sem, pair_send, pair_recv, load_sem,
 ):
     loads = [
-        pltpu.make_async_copy(psf_hbm, psf_ref, load_sem.at[0]),
-        pltpu.make_async_copy(dirty_hbm, dirty_ref, load_sem.at[1]),
+        pltpu.make_async_copy(source, target, load_sem.at[i])
+        for i, (source, target) in enumerate((
+            (tile_hbm, tile_ref), (off_hbm, off_ref), (scale_hbm, scale_ref), (amp_hbm, amp_ref),
+            (weight_hbm, weight_ref), (psf_hbm, psf_ref), (dirty_hbm, dirty_ref),
+        ))
     ]
     for load in loads:
         load.start()
@@ -125,6 +129,8 @@
     for partner in partners:
         pl.semaphore_signal(barrier, inc=1, device_id=partner, device_id_type=MESH)
 
+    for load in loads[:4]:
+        load.wait()
     records = sends_of_tiles(tile_ref[...], off_ref[...], scale_ref[...], amp_ref[...], n_ty, n_tx)
     n_yp = n_ty // 2
     for x in range(n_tx):
@@ -143,7 +149,7 @@
         stage_x.append(copy)
     own = pltpu.make_async_copy(send.at[me_x], cross.at[:, me_x, :], own_sem.at[0])
     own.start()
-    for load in loads:
+    for load in loads[4:]:
         load.wait()
     for b in range(2):
         psf[b, 0:ROWS_K, :] = psf_ref[:, b, :].astype(jnp.float32)
@@ -380,11 +386,11 @@
 
 def per_device(dirty, psf, comp_tile, comp_offset, comp_scale, comp_amp, fit_weight):
     n_band, n_ty, n_tx = (lax.axis_size(a) for a in ("band", "ty", "tx"))
-    sources = n_ty * n_tx
+    sources, listed = n_ty * n_tx, comp_tile.shape[0]
     lists = max(1, sources * SLOTS // 128)
     n_yp = n_ty // 2
     vmem = pl.BlockSpec(memory_space=pltpu.VMEM)
-    smem = pl.BlockSpec(memory_space=pltpu.SMEM)
+    hbm = pl.BlockSpec(memory_space=pltpu.HBM)
     dma = pltpu.SemaphoreType.DMA
     f32, bf16 = jnp.float32, jnp.bfloat16
     value, order, table, taylor_table, fit = pl.pallas_call(
@@ -396,14 +402,16 @@
             jax.ShapeDtypeStruct((PAD_K * HALF, 128), f32),
             jax.ShapeDtypeStruct((SIDE, SIDE), f32),
         ),
-        in_specs=[vmem] * 4 + [smem] + [pl.BlockSpec(memory_space=pltpu.HBM)] * 2,
+        in_specs=[hbm] * 7,
         out_specs=(vmem,) * 5,
         scratch_shapes=[
+            pltpu.VMEM((1, listed), jnp.int32), pltpu.VMEM((2, listed), jnp.int32),
+            pltpu.VMEM((1, listed), jnp.int32), pltpu.VMEM((TAYLOR, listed), f32),
+            pltpu.SMEM((2, TAYLOR), f32), pltpu.VMEM((2, SIDE, SIDE), f32),
+            pltpu.VMEM((ROWS_K, 2, 2 * WIDE), bf16),
             pltpu.VMEM((n_tx, n_yp, 128), f32),
             pltpu.VMEM((n_yp, n_tx, 128), f32),
             pltpu.VMEM((n_ty, n_tx, 128), f32),
-            pltpu.VMEM((2, SIDE, SIDE), f32),
-            pltpu.VMEM((ROWS_K, 2, 2 * WIDE), bf16),
             pltpu.VMEM((2, PAD_K, 2 * WIDE), f32),
             pltpu.VMEM((n_band - 1, SIDE, SIDE), bf16),
             pltpu.VMEM((n_band - 1, SIDE, SIDE), bf16),
@@ -413,15 +421,19 @@
             dma((n_tx - 1,)), dma((n_tx - 1,)),
             dma((n_ty - 1,)), dma((n_ty - 1,)),
             dma((2, n_band - 1)), dma((2, n_band - 1)),
-            dma((2,)), dma((1,)), dma((1,)), dma((2,)),
+            dma((2,)), dma((1,)), dma((1,)), dma((7,)),
         ],
         compiler_params=pltpu.CompilerParams(
             collective_id=0, has_side_effects=True, vmem_limit_bytes=24 * 1024 * 1024
         ),
     )(
-        comp_tile.T, comp_offset.T, comp_scale[None, :], comp_amp.T, fit_weight,
-        pltpu.with_memory_space_constraint(dirty, pltpu.HBM),
-        pltpu.with_memory_space_constraint(psf.transpose(1, 0, 2), pltpu.HBM),
+        *(
+            pltpu.with_memory_space_constraint(operand, pltpu.HBM)
+            for operand in (
+                comp_tile.T, comp_offset.T, comp_scale[None, :], comp_amp.T, fit_weight, dirty,
+                psf.transpose(1, 0, 2),
+            )
+        ),
     )
     residual, taylor = pl.pallas_call(
         render_kernel,
@@ -430,7 +442,7 @@
             jax.ShapeDtypeStruct((SIDE, SIDE), f32),
         ),
         in_specs=[vmem] * 6,
-        out_specs=(pl.BlockSpec(memory_space=pltpu.HBM),) * 2,
+        out_specs=(hbm,) * 2,
         scratch_shapes=[
             pltpu.VMEM(((BLOCKS - 1) * CANVAS, 128), f32) for _ in range(4)
         ] + [

time: 37.1 us -> 33.1 us (0.89)
  the two profiles are of different devices: /device:TPU:96 before, /device:TPU:16 now
where the time goes in v3:
time: 33.1 us; the launch traced here: 33.5 us
  Pallas kernels  32.8 us (99%)
  between operations  0.66 us (2%)
    pallas_call x1, Pallas kernels, per_device(): pl.pallas_call(functools.partial(exchange_kernel, n_band, n_ty, n_tx), ou...  24.9 us
    pallas_call x1, Pallas kernels, per_device(): pl.pallas_call(render_kernel, out_shape=(jax.ShapeDtypeStruct((2, SIDE, S...  7.86 us

profile of v3, /device:TPU:16, one launch (start us, length us, event | category | flops | bytes accessed | tf_op | source)
XLA Modules:
  0.0 33.5 jit_solution(957284887603483586)
XLA Ops:
  0.6 0.0 copy-start
  0.6 24.9 %shard_map.86 = (f32[72,128]{1,0:T(8,128)S(1)}, s32[16,128]{1,0:T(8,128)S(1)}, f32[1152,128]{1,0:T(8,128)S(1)}, f32[576,128]{1,0:T(8,128)S(1)}, f32[256,256]{1,0:T(8,128)S(1)}) custom-call(s32[1,128]{1,0:T(1,128)} %bitcast.13, s32[2,128]{1,0:T(2,128)} %bitcast.12, s32[1,128]{1,0:T(1,128)} %bitcast.14, f32[4,128]{1,0:T(4,128)} %bitcast.11, ...), custom_call_target="tpu_custom_call" | custom-call | tf_op jit(solution)/shard_map/pallas_call | solution.py:396
  25.6 0.0 copy-done
  25.6 7.9 %shard_map.87 = (f32[2,256,256]{2,1,0:T(8,128)}, f32[256,256]{1,0:T(8,128)}) custom-call(f32[9216]{0:T(1024)S(1)} %bitcast.8, s32[2048]{0:T(1024)S(1)} %bitcast.9, f32[1152,128]{1,0:T(8,128)S(1)} %get-tuple-element.11.table_ref, f32[576,128]{1,0:T(8,128)S(1)} %get-tuple-element.12.taylor_table_ref, f32[2,256,256]{2,1,0:T(8,128)S(1)} %copy-done, ...), custom_call_target="tpu_custom_call" | custom-call | tf_op jit(solution)/shard_map/pallas_call | solution.py:438
Async XLA Ops:
  0.6 25.0 %copy-start = (f32[2,256,256]{2,1,0:T(8,128)S(1)}, f32[2,256,256]{2,1,0:T(8,128)}, u32[]{:S(2)}) copy-start(f32[2,256,256]{2,1,0:T(8,128)} %dirty_ref.1) | copy-start | bytes 1572868

commit v4 on v3

--- a/solution.py
+++ b/solution.py
@@ -21,24 +21,24 @@
 COL_BASE = 64
 BLOCKS = 6
 CANVAS = 352
-GROUP = 8
+GROUPS = (48, 16, 8)
 MESH = pl.DeviceIdType.MESH
 
 
 def sends_of_tiles(tile, off, scale, amp, n_ty, n_tx):
     count = tile.shape[1]
-    tiles, n_yp = n_ty * n_tx, n_ty // 2
+    tiles = n_ty * n_tx
     comp_y = lax.shift_right_logical(tile, n_tx.bit_length() - 1)
     comp_x = lax.bitwise_and(tile, n_tx - 1)
     over_r = (off[0:1] + PATCH > SIDE).astype(jnp.int32)
     over_c = (off[1:2] + PATCH > SIDE).astype(jnp.int32)
     dest = lax.broadcasted_iota(jnp.int32, (tiles, count), 0)
     half = tiles // 2
-    bits = n_yp.bit_length() - 1
+    bits = n_tx.bit_length() - 1
     core = lax.shift_right_logical(dest, half.bit_length() - 1)
     inner = lax.bitwise_and(dest, half - 1)
-    dest_x = lax.shift_right_logical(inner, bits)
-    dest_y = 2 * lax.bitwise_and(inner, n_yp - 1) + core
+    dest_x = lax.bitwise_and(inner, n_tx - 1)
+    dest_y = 2 * lax.shift_right_logical(inner, bits) + core
     down, right = dest_y - comp_y, dest_x - comp_x
     touches = ((down == 0) | ((down == 1) & (over_r == 1))) & (
         (right == 0) | ((right == 1) & (over_c == 1))
@@ -132,22 +132,21 @@
     for load in loads[:4]:
         load.wait()
     records = sends_of_tiles(tile_ref[...], off_ref[...], scale_ref[...], amp_ref[...], n_ty, n_tx)
-    n_yp = n_ty // 2
-    for x in range(n_tx):
-        send[x] = records[x * n_yp:(x + 1) * n_yp]
+    for y in range(n_ty // 2):
+        send[y] = records[y * n_tx:(y + 1) * n_tx]
 
     pl.semaphore_wait(barrier, len(partners))
 
-    stage_x = []
-    for o, x in enumerate(along_x):
+    stage_y = []
+    for o, y in enumerate(along_y):
         copy = pltpu.make_async_remote_copy(
-            src_ref=send.at[x], dst_ref=cross.at[:, me_x, :],
-            send_sem=x_send.at[o], recv_sem=x_recv.at[o],
-            device_id=(me_b, me_y, x), device_id_type=MESH,
+            src_ref=send.at[y // 2], dst_ref=cross.at[me_y],
+            send_sem=y_send.at[o], recv_sem=y_recv.at[o],
+            device_id=(me_b, y, me_x), device_id_type=MESH,
         )
         copy.start()
-        stage_x.append(copy)
-    own = pltpu.make_async_copy(send.at[me_x], cross.at[:, me_x, :], own_sem.at[0])
+        stage_y.append(copy)
+    own = pltpu.make_async_copy(send.at[me_y // 2], cross.at[me_y], own_sem.at[0])
     own.start()
     for load in loads[4:]:
         load.wait()
@@ -193,18 +192,18 @@
             copies.append(copy)
 
     own.wait()
-    for copy in stage_x:
+    for copy in stage_y:
         copy.wait_recv()
-    stage_y = []
-    for o, y in enumerate(along_y):
+    stage_x = []
+    for o, x in enumerate(along_x):
         copy = pltpu.make_async_remote_copy(
-            src_ref=cross.at[y // 2], dst_ref=got.at[me_y],
-            send_sem=y_send.at[o], recv_sem=y_recv.at[o],
-            device_id=(me_b, y, me_x), device_id_type=MESH,
+            src_ref=cross.at[:, x, :], dst_ref=got.at[:, me_x, :],
+            send_sem=x_send.at[o], recv_sem=x_recv.at[o],
+            device_id=(me_b, me_y, x), device_id_type=MESH,
         )
         copy.start()
-        stage_y.append(copy)
-    own = pltpu.make_async_copy(cross.at[me_y // 2], got.at[me_y], own_sem.at[1])
+        stage_x.append(copy)
+    own = pltpu.make_async_copy(cross.at[:, me_x, :], got.at[:, me_x, :], own_sem.at[1])
     own.start()
 
     for copy in stage_t:
@@ -219,8 +218,18 @@
     )
     pair.start()
 
+    pair.wait_recv()
+    first, last = piece(tab_own.at[0], 0), piece(tab_own.at[1], 0)
+    for step in range(HALF):
+        taylor_table_ref[pl.ds(step, PAD_K, stride=HALF), :] = unrolled(first, last, lane24, step)
+
+    fit_ref[...] = w0 * dirty_ref[0] + w1 * dirty_ref[1]
+    for copy in stage_f:
+        copy.wait_recv()
+    for o in range(n_band - 1):
+        fit_ref[...] += fit_got[o].astype(jnp.float32)
     own.wait()
-    for copy in stage_y:
+    for copy in stage_x:
         copy.wait_recv()
     sources = n_ty * n_tx
     slots = jnp.concatenate([got[y] for y in range(n_ty)], axis=0)
@@ -264,16 +273,6 @@
         list_ref[i:i + 1, :] = index.astype(jnp.int32)
     list_ref[lists:lists + 1, :] = end[sources - 1:sources].astype(jnp.int32)
 
-    pair.wait_recv()
-    first, last = piece(tab_own.at[0], 0), piece(tab_own.at[1], 0)
-    for step in range(HALF):
-        taylor_table_ref[pl.ds(step, PAD_K, stride=HALF), :] = unrolled(first, last, lane24, step)
-
-    fit_ref[...] = w0 * dirty_ref[0] + w1 * dirty_ref[1]
-    for copy in stage_f:
-        copy.wait_recv()
-    for o in range(n_band - 1):
-        fit_ref[...] += fit_got[o].astype(jnp.float32)
     for copy in stage_x + stage_y + stage_t + stage_f + [pair]:
         copy.wait_send()
 
@@ -302,9 +301,9 @@
     half_lane = lax.bitwise_and(lax.broadcasted_iota(jnp.int32, (HALF, 128), 1), 63)
     count = list_ref[list_ref.shape[0] - 1024]
 
-    def step(index, carry):
-        for g in range(GROUP):
-            slot = list_ref[index * GROUP + g]
+    def step(first_of_all, group, index, carry):
+        for g in range(group):
+            slot = list_ref[first_of_all + index * group + g]
             packed = amp_ref[slot].astype(jnp.int32)
             amps = [amp_ref[slot + 4 + t] for t in range(TAYLOR)]
             first = lax.bitwise_and(packed, 2047)
@@ -335,7 +334,12 @@
                 pltpu.store(here, value, mask=mask)
         return carry
 
-    lax.fori_loop(0, (count + GROUP - 1) // GROUP, step, 0)
+    done = 0
+    for group in GROUPS:
+        left = count - done + (group - 1 if group == GROUPS[-1] else 0)
+        turns = left // group
+        lax.fori_loop(0, turns, functools.partial(step, done, group), 0)
+        done = done + turns * group
 
     rows = 64
     lower = lax.broadcasted_iota(jnp.int32, (rows, 128), 1) < 64
@@ -388,7 +392,6 @@
     n_band, n_ty, n_tx = (lax.axis_size(a) for a in ("band", "ty", "tx"))
     sources, listed = n_ty * n_tx, comp_tile.shape[0]
     lists = max(1, sources * SLOTS // 128)
-    n_yp = n_ty // 2
     vmem = pl.BlockSpec(memory_space=pltpu.VMEM)
     hbm = pl.BlockSpec(memory_space=pltpu.HBM)
     dma = pltpu.SemaphoreType.DMA
@@ -409,8 +412,8 @@
             pltpu.VMEM((1, listed), jnp.int32), pltpu.VMEM((TAYLOR, listed), f32),
             pltpu.SMEM((2, TAYLOR), f32), pltpu.VMEM((2, SIDE, SIDE), f32),
             pltpu.VMEM((ROWS_K, 2, 2 * WIDE), bf16),
-            pltpu.VMEM((n_tx, n_yp, 128), f32),
-            pltpu.VMEM((n_yp, n_tx, 128), f32),
+            pltpu.VMEM((n_ty // 2, n_tx, 128), f32),
+            pltpu.VMEM((n_ty, n_tx, 128), f32),
             pltpu.VMEM((n_ty, n_tx, 128), f32),
             pltpu.VMEM((2, PAD_K, 2 * WIDE), f32),
             pltpu.VMEM((n_band - 1, SIDE, SIDE), bf16),

time: 33.1 us -> 32.7 us (0.988)
  the two profiles are of different devices: /device:TPU:16 before, /device:TPU:1 now
where the time goes in v4:
time: 32.7 us; the launch traced here: 32.8 us
  Pallas kernels  32.2 us (98%)
  between operations  0.66 us (2%)
    pallas_call x1, Pallas kernels, per_device(): pl.pallas_call(functools.partial(exchange_kernel, n_band, n_ty, n_tx), ou...  25.3 us
    pallas_call x1, Pallas kernels, per_device(): pl.pallas_call(render_kernel, out_shape=(jax.ShapeDtypeStruct((2, SIDE, S...  6.83 us

profile of v4, /device:TPU:1, one launch (start us, length us, event | category | flops | bytes accessed | tf_op | source)
XLA Modules:
  0.0 32.8 jit_solution(16070474792175755700)
XLA Ops:
  0.6 0.0 copy-start
  0.6 25.3 %shard_map.86 = (f32[72,128]{1,0:T(8,128)S(1)}, s32[16,128]{1,0:T(8,128)S(1)}, f32[1152,128]{1,0:T(8,128)S(1)}, f32[576,128]{1,0:T(8,128)S(1)}, f32[256,256]{1,0:T(8,128)S(1)}) custom-call(s32[1,128]{1,0:T(1,128)} %bitcast.13, s32[2,128]{1,0:T(2,128)} %bitcast.12, s32[1,128]{1,0:T(1,128)} %bitcast.14, f32[4,128]{1,0:T(4,128)} %bitcast.11, ...), custom_call_target="tpu_custom_call" | custom-call | tf_op jit(solution)/shard_map/pallas_call | solution.py:399
  26.0 0.0 copy-done
  26.0 6.8 %shard_map.87 = (f32[2,256,256]{2,1,0:T(8,128)}, f32[256,256]{1,0:T(8,128)}) custom-call(f32[9216]{0:T(1024)S(1)} %bitcast.8, s32[2048]{0:T(1024)S(1)} %bitcast.9, f32[1152,128]{1,0:T(8,128)S(1)} %get-tuple-element.11.table_ref, f32[576,128]{1,0:T(8,128)S(1)} %get-tuple-element.12.taylor_table_ref, f32[2,256,256]{2,1,0:T(8,128)S(1)} %copy-done, ...), custom_call_target="tpu_custom_call" | custom-call | tf_op jit(solution)/shard_map/pallas_call | solution.py:441
Async XLA Ops:
  0.6 25.4 %copy-start = (f32[2,256,256]{2,1,0:T(8,128)S(1)}, f32[2,256,256]{2,1,0:T(8,128)}, u32[]{:S(2)}) copy-start(f32[2,256,256]{2,1,0:T(8,128)} %dirty_ref.1) | copy-start | bytes 1572868
